TPU v7x, 32 devices: a whole 2x2x4 slice. The times are simulated.
32 devices in a mesh: dp: 16 (over z, y, core), tensor: 2 (over x).
Axes of the slice: x: 2, y: 2, z: 4, core: 2. Of those that a mesh axis runs over, the one named last changes fastest.
Arguments:
- block_in: bfloat16 [16, 1024, 1024], P('dp', 'tensor'), may hold values from -50 to 50
- valid_count: int32 [16], P('dp'), may hold values from 512 to 1024, as said below
- vectors: float32 [14, 1024], P(None, ('dp', 'tensor')), may hold values from -2 to 2
- qkv_weight: bfloat16 [3, 1024, 1024], P(None, 'dp', 'tensor'), may hold values from -1.5 to 1.5
- out_weight: bfloat16 [1024, 1024], P('tensor', 'dp'), may hold values from -1.5 to 1.5
- up_weight: bfloat16 [1024, 4096], P('dp', 'tensor'), may hold values from -0.1875 to 0.1875
- down_weight: bfloat16 [4096, 1024], P('tensor', 'dp'), may hold values from -0.09375 to 0.09375
- cotangent: bfloat16 [16, 1024, 1024], P('dp', 'tensor'), may hold values from -6 to 6
Outputs:
- block_out: bfloat16 [16, 1024, 1024], P('dp', 'tensor')
- grad_input: float32 [16, 1024, 1024], P('dp', 'tensor')
- grad_vectors: float32 [14, 1024], P(None, ('dp', 'tensor'))
- grad_qkv: float32 [3, 1024, 1024], P(None, 'dp', 'tensor')
- grad_proj: float32 [1024, 1024], P('tensor', 'dp')
- grad_up: float32 [1024, 4096], P('dp', 'tensor')
- grad_down: float32 [4096, 1024], P('tensor', 'dp')
Inputs may be any that keep to these rules, and one draw needn't show every extreme that they name: Keys from position valid_count on are masked in their image; some image has all 1024 tokens valid.
All inputs are finite; a program needn't handle non-finite values.
Results may differ from a plain program's by a relative error of at most 0.019.
Values may be sent and summed in bfloat16 or wider, within the bound.
A program may use at most 192 MiB of HBM per device.

v0:
```python
import jax
import jax.numpy as jnp
from jax import lax
from jax.sharding import PartitionSpec as P

FF = 4096
HEAD = 64
NORM_EPS = 1e-06
ROOT_HALF = 0.7071067811865476
INV_ROOT_TAU = 0.3989422804014327
MASKED = -1e30


def layer_norm(values):
    center = values - jnp.mean(values, axis=-1, keepdims=True)
    inverse = lax.rsqrt(jnp.mean(center * center, axis=-1, keepdims=True) + NORM_EPS)
    return (center * inverse, inverse)


def norm_back(grad_hat, normed, inverse):
    first_mean = jnp.mean(grad_hat, axis=-1, keepdims=True)
    second_mean = jnp.mean(grad_hat * normed, axis=-1, keepdims=True)
    return inverse * (grad_hat - first_mean - normed * second_mean)


def gelu_pair(hidden):
    cumul = 0.5 * (1.0 + jax.scipy.special.erf(hidden * ROOT_HALF))
    density = jnp.exp(-0.5 * hidden * hidden) * INV_ROOT_TAU
    return (hidden * cumul, cumul + hidden * density)


def matmul(left_side, right_side):
    return jnp.dot(left_side, right_side, preferred_element_type=jnp.float32)


def times_transposed(left_side, right_side):
    return lax.dot_general(
        left_side, right_side, (((1,), (1,)), ((), ())), preferred_element_type=jnp.float32
    )


def transposed_times(left_side, right_side):
    return lax.dot_general(
        left_side, right_side, (((0,), (0,)), ((), ())), preferred_element_type=jnp.float32
    )


def masked_scores(queries, key_rows, visible, score_scale):
    scores = (
        jnp.einsum("qhe,khe->hqk", queries, key_rows, preferred_element_type=jnp.float32)
        * score_scale
    )
    return jnp.where(visible[None, None, :], scores, MASKED)


def attend(queries, key_rows, value_rows, visible, score_scale):
    scores = masked_scores(queries, key_rows, visible, score_scale)
    row_max = jnp.max(scores, axis=-1, keepdims=True)
    log_total = row_max + jnp.log(jnp.sum(jnp.exp(scores - row_max), axis=-1, keepdims=True))
    weights_low = jnp.exp(scores - log_total).astype(jnp.bfloat16)
    mixed = jnp.einsum("hqk,khe->qhe", weights_low, value_rows, preferred_element_type=jnp.float32)
    return (mixed.astype(jnp.bfloat16), log_total)


def attend_back(queries, key_rows, value_rows, mixed, grad_mixed, log_total, visible, score_scale):
    probs = jnp.exp(masked_scores(queries, key_rows, visible, score_scale) - log_total)
    probs_low = probs.astype(jnp.bfloat16)
    grad_values = jnp.einsum(
        "hqk,qhe->khe", probs_low, grad_mixed, preferred_element_type=jnp.float32
    )
    grad_probs = jnp.einsum(
        "qhe,khe->hqk", grad_mixed, value_rows, preferred_element_type=jnp.float32
    )
    delta = jnp.einsum("qhe,qhe->hq", grad_mixed, mixed, preferred_element_type=jnp.float32)[
        :, :, None
    ]
    grad_scores = (probs * (grad_probs - delta)).astype(jnp.bfloat16)
    grad_queries = score_scale * jnp.einsum(
        "hqk,khe->qhe", grad_scores, key_rows, preferred_element_type=jnp.float32
    )
    grad_keys = score_scale * jnp.einsum(
        "hqk,qhe->khe", grad_scores, queries, preferred_element_type=jnp.float32
    )
    return (grad_queries, grad_keys, grad_values)


def gather_rows(shard_low):
    return lax.all_gather(shard_low, "tensor", axis=0, tiled=True)


def gather_cotangent(shard_low):
    return lax.all_gather(shard_low, "tensor", axis=0, tiled=True)


def pair_sum(factor_pairs, product):
    running = None
    for left_side, right_side in factor_pairs:
        addend = product(left_side, right_side)
        running = addend if running is None else running + addend
    return running


def branch_rows(factor_pairs):
    return lax.psum_scatter(
        pair_sum(factor_pairs, matmul).astype(jnp.bfloat16),
        "tensor",
        scatter_dimension=0,
        tiled=True,
    ).astype(jnp.float32)


def back_rows(factor_pairs):
    return lax.psum_scatter(
        pair_sum(factor_pairs, times_transposed).astype(jnp.bfloat16),
        "tensor",
        scatter_dimension=0,
        tiled=True,
    ).astype(jnp.float32)


def local(
    block_in, valid_count, vectors, qkv_weight, out_weight, up_weight, down_weight, cotangent
):
    params = lax.all_gather(vectors, ("dp", "tensor"), axis=1, tiled=True)
    qkv_full, out_full, up_full, down_full = (
        lax.all_gather(qkv_weight, "dp", axis=1, tiled=True),
        lax.all_gather(out_weight, "dp", axis=1, tiled=True),
        lax.all_gather(up_weight, "dp", axis=0, tiled=True),
        lax.all_gather(down_weight, "dp", axis=1, tiled=True),
    )
    model_width = params.shape[1]
    local_width = qkv_full.shape[2]
    local_units = up_full.shape[1]
    local_heads = local_width // HEAD
    shard_rows = block_in.shape[1]
    seq_len = shard_rows * lax.axis_size("tensor")
    tensor_rank = lax.axis_index("tensor")
    score_scale = HEAD ** (-0.5)
    (
        gain_one,
        shift_one,
        query_bias_all,
        value_bias_all,
        bias_out,
        scale_one,
        gain_two,
        shift_two,
        bias_down,
        scale_two,
    ) = params[:10]
    bias_query = lax.dynamic_slice_in_dim(query_bias_all, tensor_rank * local_width, local_width)
    bias_value = lax.dynamic_slice_in_dim(value_bias_all, tensor_rank * local_width, local_width)
    bias_up = lax.dynamic_slice_in_dim(
        params[10:].reshape(-1), tensor_rank * local_units, local_units
    )
    positions = lax.iota(jnp.int32, seq_len)
    zero_row = jnp.zeros((model_width,), jnp.float32)
    input_rows = block_in[0].astype(jnp.float32)
    normed_one, inverse_one = layer_norm(input_rows)
    hidden_one = gather_rows((normed_one * gain_one + shift_one).astype(jnp.bfloat16))
    queries = (
        (matmul(hidden_one, qkv_full[0]) + bias_query)
        .astype(jnp.bfloat16)
        .reshape(seq_len, local_heads, HEAD)
    )
    key_rows = (
        matmul(hidden_one, qkv_full[1]).astype(jnp.bfloat16).reshape(seq_len, local_heads, HEAD)
    )
    value_rows = (
        (matmul(hidden_one, qkv_full[2]) + bias_value)
        .astype(jnp.bfloat16)
        .reshape(seq_len, local_heads, HEAD)
    )
    visible = positions < valid_count[0]
    mixed, log_total = attend(queries, key_rows, value_rows, visible, score_scale)
    mixed_flat = mixed.reshape(seq_len, local_width)
    branch_one = branch_rows(((mixed_flat, out_full),)) + bias_out
    middle = input_rows + scale_one * branch_one
    normed_two, inverse_two = layer_norm(middle)
    hidden_two = gather_rows((normed_two * gain_two + shift_two).astype(jnp.bfloat16))
    activated, gelu_slope = gelu_pair(matmul(hidden_two, up_full) + bias_up)
    act_low = activated.astype(jnp.bfloat16)
    branch_two = branch_rows(((act_low, down_full),)) + bias_down
    out_list = [(middle + scale_two * branch_two).astype(jnp.bfloat16)]
    grad_rows = cotangent[0].astype(jnp.float32)
    grad_scale_two = jnp.sum(grad_rows * branch_two, axis=0)
    grad_bias_down = jnp.sum(grad_rows * scale_two, axis=0)
    grad_branch_two = gather_cotangent((grad_rows * scale_two).astype(jnp.bfloat16))
    grad_down = transposed_times(act_low, grad_branch_two)
    grad_pre = times_transposed(grad_branch_two, down_full) * gelu_slope
    grad_bias_up = jnp.sum(grad_pre, axis=0)
    grad_pre_low = grad_pre.astype(jnp.bfloat16)
    grad_up = transposed_times(hidden_two, grad_pre_low)
    grad_hidden_two = back_rows(((grad_pre_low, up_full),))
    grad_gain_two = jnp.sum(grad_hidden_two * normed_two, axis=0)
    grad_shift_two = jnp.sum(grad_hidden_two, axis=0)
    grad_middle = grad_rows + norm_back(grad_hidden_two * gain_two, normed_two, inverse_two)
    grad_scale_one = jnp.sum(grad_middle * branch_one, axis=0)
    grad_bias_out = jnp.sum(grad_middle * scale_one, axis=0)
    grad_branch_one = gather_cotangent((grad_middle * scale_one).astype(jnp.bfloat16))
    grad_proj_sum = transposed_times(mixed_flat, grad_branch_one)
    grad_mixed = (
        times_transposed(grad_branch_one, out_full)
        .astype(jnp.bfloat16)
        .reshape(seq_len, local_heads, HEAD)
    )
    grad_queries, grad_keys, grad_values = attend_back(
        queries, key_rows, value_rows, mixed, grad_mixed, log_total, visible, score_scale
    )
    grad_queries = grad_queries.reshape(seq_len, local_width)
    grad_keys = grad_keys.reshape(seq_len, local_width)
    grad_values = grad_values.reshape(seq_len, local_width)
    grad_bias_query = jnp.sum(grad_queries, axis=0)
    grad_bias_value = jnp.sum(grad_values, axis=0)
    query_low = grad_queries.astype(jnp.bfloat16)
    key_low = grad_keys.astype(jnp.bfloat16)
    value_low = grad_values.astype(jnp.bfloat16)
    grad_qkv_sum = jnp.stack(
        [
            transposed_times(hidden_one, query_low),
            transposed_times(hidden_one, key_low),
            transposed_times(hidden_one, value_low),
        ]
    )
    grad_hidden_one = back_rows(
        ((query_low, qkv_full[0]), (key_low, qkv_full[1]), (value_low, qkv_full[2]))
    )
    grad_gain_one = jnp.sum(grad_hidden_one * normed_one, axis=0)
    grad_shift_one = jnp.sum(grad_hidden_one, axis=0)
    grad_list = [grad_middle + norm_back(grad_hidden_one * gain_one, normed_one, inverse_one)]
    placed_query = lax.dynamic_update_slice_in_dim(
        zero_row, grad_bias_query, tensor_rank * local_width, 0
    )
    placed_value = lax.dynamic_update_slice_in_dim(
        zero_row, grad_bias_value, tensor_rank * local_width, 0
    )
    placed_up = lax.dynamic_update_slice_in_dim(
        jnp.zeros((FF,), jnp.float32), grad_bias_up, tensor_rank * local_units, 0
    )
    image_params = jnp.concatenate(
        [
            jnp.stack(
                [
                    grad_gain_one,
                    grad_shift_one,
                    placed_query,
                    placed_value,
                    grad_bias_out,
                    grad_scale_one,
                    grad_gain_two,
                    grad_shift_two,
                    grad_bias_down,
                    grad_scale_two,
                ]
            ),
            placed_up.reshape(-1, model_width),
        ],
        axis=0,
    )
    owned_qkv, owned_proj, owned_up, owned_down = (
        lax.psum_scatter(
            grad_qkv_sum.astype(jnp.bfloat16), "dp", scatter_dimension=1, tiled=True
        ).astype(jnp.float32),
        lax.psum_scatter(
            grad_proj_sum.astype(jnp.bfloat16), "dp", scatter_dimension=1, tiled=True
        ).astype(jnp.float32),
        lax.psum_scatter(
            grad_up.astype(jnp.bfloat16), "dp", scatter_dimension=0, tiled=True
        ).astype(jnp.float32),
        lax.psum_scatter(
            grad_down.astype(jnp.bfloat16), "dp", scatter_dimension=1, tiled=True
        ).astype(jnp.float32),
    )
    owned_params = lax.psum_scatter(image_params, ("dp", "tensor"), scatter_dimension=1, tiled=True)
    return (
        jnp.stack(out_list),
        jnp.stack(grad_list),
        owned_params,
        owned_qkv,
        owned_proj,
        owned_up,
        owned_down,
    )


def solution(mesh):
    placed = (
        P("dp", "tensor", None),
        P("dp"),
        P(None, ("dp", "tensor")),
        P(None, "dp", "tensor"),
        P("tensor", "dp"),
        P("dp", "tensor"),
        P("tensor", "dp"),
        P("dp", "tensor", None),
    )
    return jax.shard_map(
        local,
        mesh=mesh,
        in_specs=placed,
        out_specs=(
            P("dp", "tensor", None),
            P("dp", "tensor", None),
            P(None, ("dp", "tensor")),
            P(None, "dp", "tensor"),
            P("tensor", "dp"),
            P("dp", "tensor"),
            P("tensor", "dp"),
        ),
        check_vma=False,
    )
```

profile of v0, /device:TPU:0, one launch (start us, length us, event | category | flops | bytes accessed | tf_op | source)
XLA Modules:
  0.0 1073.9 jit_solution(8662764909699897277)
XLA Ops:
  7.2 71.4 %all-gather = f32[32,32,14]{1,2,0:T(8,128)S(1)} all-gather(f32[1,32,14]{1,2,0:T(8,128)} %bitcast.230), channel_id=1, replica_groups=mesh['dp'=16,'tensor'=2] {'dp','tensor'}, dimensions={0}, use_global_device_ids=true | all-gather | bytes 59136 | tf_op jit(solution)/shard_map/all_gather | solution.py:124
  84.5 26.9 %all-gather.10.cloned.1.call-done = bf16[1024,1024]{1,0:T(8,128)(2,1)} async-done(((bf16[512,1024]{1,0:T(8,128)(2,1)}), bf16[1024,1024]{1,0:T(8,128)(2,1)}) %all-gather.10.cloned.1.call-update) | async-done | bytes 2097168 | tf_op jit(solution)/shard_map/all_gather | solution.py:88
  111.4 47.7 %all-gather.12.cloned.1.call-done = bf16[3,1024,512]{2,1,0:T(8,128)(2,1)} async-done(((bf16[3,64,512]{2,1,0:T(8,128)(2,1)}), bf16[3,1024,512]{2,1,0:T(8,128)(2,1)}) %all-gather.12.cloned.1.call-update) | async-done | bytes 3145744 | tf_op jit(solution)/shard_map/all_gather | solution.py:126
  164.0 14.1 %fusion.1 = (f32[8,1024]{1,0:T(8,128)S(1)}, f32[8,1024,1024]{1,2,0:T(8,128)}) fusion(pred[1024]{0:T(1024)(128)(4,1)S(1)} %iota_compare_fusion, bf16[1024,8,64]{0,2,1:T(8,128)(2,1)S(1)} %bitcast.181, bf16[1024,8,64]{0,2,1:T(8,128)(2,1)S(1)} %bitcast.179), kind=kOutput, calls=%fused_computation.5 | convolution fusion | flops 1098899456 | bytes 35685376 | tf_op jit(solution)/shard_map/qhe,khe->hqk/dot_general | solution.py:50
  178.1 15.1 %exponential_reduce_fusion = f32[8,1024]{1,0:T(8,128)S(1)} fusion(f32[8,1024,1024]{1,2,0:T(8,128)} %get-tuple-element.34, f32[8,1024]{1,0:T(8,128)S(1)} %get-tuple-element.33, pred[1024]{0:T(1024)(128)(4,1)S(1)} %iota_compare_fusion), kind=kLoop, calls=%fused_computation.2 | loop fusion | flops 33546240 | bytes 33620992 | tf_op jit(solution)/shard_map/reduce_sum | solution.py:59
  193.2 5.3 copy-done
  198.5 9.6 fusion
  211.9 8.8 convolution_convert_fusion.10
  225.7 29.8 %reduce-scatter.12.cloned.1.call-done = bf16[512,1024]{1,0:T(8,128)(2,1)} async-done(((bf16[1024,1024]{1,0:T(8,128)(2,1)}), bf16[512,1024]{1,0:T(8,128)(2,1)}) %reduce-scatter.12.cloned.1.call-update) | async-done | bytes 1048592 | tf_op jit(solution)/shard_map/reduce_scatter | solution.py:104
  262.2 45.6 %all-gather.18.cloned.1.call-done = bf16[1024,2048]{1,0:T(8,128)(2,1)} async-done(((bf16[64,2048]{1,0:T(8,128)(2,1)}), bf16[1024,2048]{1,0:T(8,128)(2,1)}) %all-gather.18.cloned.1.call-update) | async-done | bytes 4194320 | tf_op jit(solution)/shard_map/all_gather | solution.py:128
  307.9 33.6 %all-gather.16.cloned.1.call-done = bf16[1024,1024]{1,0:T(8,128)(2,1)} async-done(((bf16[512,1024]{1,0:T(8,128)(2,1)}), bf16[1024,1024]{1,0:T(8,128)(2,1)}) %all-gather.16.cloned.1.call-update) | async-done | bytes 2097168 | tf_op jit(solution)/shard_map/all_gather | solution.py:88
  341.5 10.1 multiply_convert_fusion.1
  351.6 25.1 %all-gather.22.cloned.1.call-done = bf16[1024,1024]{1,0:T(8,128)(2,1)} async-done(((bf16[512,1024]{1,0:T(8,128)(2,1)}), bf16[1024,1024]{1,0:T(8,128)(2,1)}) %all-gather.22.cloned.1.call-update) | async-done | bytes 2097168 | tf_op jit(solution)/shard_map/all_gather | solution.py:92
  376.7 52.6 %all-gather.20.cloned.1.call-done = bf16[2048,1024]{0,1:T(8,128)(2,1)} async-done(((bf16[2048,64]{0,1:T(8,128)(2,1)}), bf16[2048,1024]{0,1:T(8,128)(2,1)}) %all-gather.20.cloned.1.call-update) | async-done | bytes 4194320 | tf_op jit(solution)/shard_map/all_gather | solution.py:129
  429.3 10.8 %fusion.50 = (f32[2048]{0:T(1024)S(1)}, bf16[1024,2048]{1,0:T(8,128)(2,1)S(1)}) fusion(f32[1024,2048]{1,0:T(8,128)} %get-tuple-element.36, f32[2048]{0:T(1024)S(1)} %dynamic_slice.11, bf16[1024,1024]{1,0:T(8,128)(2,1)} %all-gather.22.cloned.1.call-done, bf16[2048,1024]{0,1:T(8,128)(2,1)} %all-gather.20.cloned.1.call-done), kind=kOutput, calls=%fused_computation.115 | convolution fusion | flops 4320131072 | bytes 18890752 | tf_op jit(solution)/shard_map/dot_general | solution.py:37
  442.1 5.7 fusion.39
  447.9 9.3 convolution_convert_fusion.2
  457.4 21.0 %reduce-scatter.16.cloned.1.call-done = bf16[512,1024]{1,0:T(8,128)(2,1)} async-done(((bf16[1024,1024]{1,0:T(8,128)(2,1)}), bf16[512,1024]{1,0:T(8,128)(2,1)}) %reduce-scatter.16.cloned.1.call-update) | async-done | bytes 1048592 | tf_op jit(solution)/shard_map/reduce_scatter | solution.py:113
  480.9 31.5 %reduce-scatter.14.cloned.1.call-done = bf16[512,1024]{1,0:T(8,128)(2,1)} async-done(((bf16[1024,1024]{1,0:T(8,128)(2,1)}), bf16[512,1024]{1,0:T(8,128)(2,1)}) %reduce-scatter.14.cloned.1.call-update) | async-done | bytes 1048592 | tf_op jit(solution)/shard_map/reduce_scatter | solution.py:104
  512.5 4.4 multiply_reduce_fusion
  519.5 33.2 %all-gather.24.cloned.1.call-done = bf16[1024,1024]{1,0:T(8,128)(2,1)} async-done(((bf16[512,1024]{1,0:T(8,128)(2,1)}), bf16[1024,1024]{1,0:T(8,128)(2,1)}) %all-gather.24.cloned.1.call-update) | async-done | bytes 2097168 | tf_op jit(solution)/shard_map/all_gather | solution.py:92
  556.6 12.3 %bitcast_convert_fusion = (bf16[1024,8,64]{0,2,1:T(8,128)(2,1)}, f32[8,64,1024]{2,1,0:T(8,128)S(1)}) fusion(bf16[1024,8,64]{0,2,1:T(8,128)(2,1)} %bitcast.194, bf16[8,1024,1024]{1,2,0:T(8,128)(2,1)} %fusion), kind=kOutput, calls=%fused_computation.58 | convolution fusion | flops 1074266112 | bytes 20971520 | tf_op jit(solution)/shard_map/hqk,qhe->khe/dot_general | solution.py:68
  568.9 21.1 %multiply_convert_fusion = bf16[8,1024,1024]{1,2,0:T(8,128)(2,1)} fusion(f32[8,1024,1024]{1,2,0:T(8,128)} %get-tuple-element.34, f32[8,1024]{1,0:T(8,128)S(1)} %get-tuple-element.37, f32[8,1024]{1,0:T(8,128)S(1)} %log_add_fusion, pred[1024]{0:T(1024)(128)(4,1)S(1)} %iota_compare_fusion, bf16[1024,8,64]{0,2,1:T(8,128)(2,1)} %bitcast.195, ...), kind=kOutput, calls=%fused_computation | convolution fusion | flops 1124073472 | bytes 52495360 | tf_op jit(solution)/shard_map/qhe,khe->hqk/dot_general | solution.py:71
  590.0 12.3 %multiply_convert_fusion.2 = bf16[8,64,1024]{2,1,0:T(8,128)(2,1)} fusion(bf16[1024,8,64]{0,2,1:T(8,128)(2,1)} %bitcast.182, bf16[8,1024,1024]{1,2,0:T(8,128)(2,1)} %multiply_convert_fusion), kind=kOutput, calls=%fused_computation.64 | convolution fusion | flops 1074790400 | bytes 18874368 | tf_op jit(solution)/shard_map/hqk,qhe->khe/dot_general | solution.py:81
  602.3 10.6 bitcast_convert_fusion.1
  618.6 9.5 convolution_convert_fusion.1
  628.1 9.4 convolution_convert_fusion
  658.0 68.9 %reduce-scatter.24.cloned.1.call-done = bf16[64,2048]{1,0:T(8,128)(2,1)} async-done(((bf16[1024,2048]{1,0:T(8,128)(2,1)}), bf16[64,2048]{1,0:T(8,128)(2,1)}) %reduce-scatter.24.cloned.1.call-update) | async-done | bytes 262160 | tf_op jit(solution)/shard_map/reduce_scatter | solution.py:267
  728.7 73.8 %reduce-scatter.26.cloned.1.call-done = bf16[2048,64]{0,1:T(8,128)(2,1)} async-done(((bf16[2048,1024]{0,1:T(8,128)(2,1)}), bf16[2048,64]{0,1:T(8,128)(2,1)}) %reduce-scatter.26.cloned.1.call-update) | async-done | bytes 262160 | tf_op jit(solution)/shard_map/reduce_scatter | solution.py:270
  804.2 58.3 %reduce-scatter.22.cloned.1.call-done = bf16[512,64]{0,1:T(8,128)(2,1)} async-done(((bf16[512,1024]{0,1:T(8,128)(2,1)}), bf16[512,64]{0,1:T(8,128)(2,1)}) %reduce-scatter.22.cloned.1.call-update) | async-done | bytes 65552 | tf_op jit(solution)/shard_map/reduce_scatter | solution.py:264
  867.4 132.2 %reduce-scatter.28.cloned.1.call-done = f32[32,14]{1,0:T(8,128)} async-done(((f32[1024,14]{1,0:T(8,128)}), f32[32,14]{1,0:T(8,128)}) %reduce-scatter.28.cloned.1.call-update) | async-done | bytes 1808
  1000.9 64.6 %reduce-scatter.20.cloned.1.call-done = bf16[3,64,512]{2,1,0:T(8,128)(2,1)} async-done(((bf16[3,1024,512]{2,1,0:T(8,128)(2,1)}), bf16[3,64,512]{2,1,0:T(8,128)(2,1)}) %reduce-scatter.20.cloned.1.call-update) | async-done | bytes 196624 | tf_op jit(solution)/shard_map/reduce_scatter | solution.py:261
  (156 shorter events, 74.1 us)
Async XLA Ops:
  7.2 73.2 %copy-start.1 = (bf16[1,512,1024]{2,1,0:T(8,128)(2,1)S(1)}, bf16[1,512,1024]{2,1,0:T(8,128)(2,1)}, u32[]{:S(2)}) copy-start(bf16[1,512,1024]{2,1,0:T(8,128)(2,1)} %param.8) | copy-start | bytes 3145732
  7.2 104.2 %all-gather.10.cloned.1.call-start = ((), (), s32[]{:S(2)}) async-start(), calls=%async_computation.9 | async-start | bytes 3145728 | tf_op jit(solution)/shard_map/all_gather | solution.py:88
  78.9 3.3 copy-start.20
  80.8 81.6 %copy-start.24 = (f32[512]{0:T(512)}, f32[512]{0:T(512)S(1)}, u32[]{:S(2)}) copy-start(f32[512]{0:T(512)S(1)} %add_rsqrt_fusion.1) | copy-start | bytes 6148
  82.3 76.8 %all-gather.12.cloned.1.call-start = ((), (), s32[]{:S(2)}) async-start(), calls=%async_computation.10 | async-start | bytes 3342336 | tf_op jit(solution)/shard_map/all_gather | solution.py:126
  83.0 137.7 %all-gather.14.cloned.1.call-start = ((), (), s32[]{:S(2)}) async-start(), calls=%async_computation.11 | async-start | bytes 1114112 | tf_op jit(solution)/shard_map/all_gather | solution.py:127
  83.8 171.7 %reduce-scatter.12.cloned.1.call-start = ((), (), s32[]{:S(2)}) async-start(), calls=%async_computation.12 | async-start | bytes 3145728 | tf_op jit(solution)/shard_map/reduce_scatter | solution.py:104
  159.1 3.3 copy-start.18
  159.1 3.5 copy-start.27
  163.9 14.1 %copy-start.6 = (bf16[1024,512]{0,1:T(8,128)(2,1)}, bf16[1024,512]{0,1:T(8,128)(2,1)S(1)}, u32[]{:S(2)}) copy-start(bf16[1024,512]{0,1:T(8,128)(2,1)S(1)} %add_convert_fusion.3) | copy-start | bytes 3145732
  178.1 20.5 %copy-start = (f32[8,1024,1024]{1,2,0:T(8,128)S(1)}, f32[8,1024,1024]{1,2,0:T(8,128)}, u32[]{:S(2)}) copy-start(f32[8,1024,1024]{1,2,0:T(8,128)} %get-tuple-element.34) | copy-start | bytes 100663296
  220.7 4.3 copy-start.10
  225.0 82.8 %all-gather.18.cloned.1.call-start = ((), (), s32[]{:S(2)}) async-start(), calls=%async_computation.14 | async-start | bytes 4456448 | tf_op jit(solution)/shard_map/all_gather | solution.py:128
  225.6 115.9 %all-gather.16.cloned.1.call-start = ((), (), s32[]{:S(2)}) async-start(), calls=%async_computation.13 | async-start | bytes 3145728 | tf_op jit(solution)/shard_map/all_gather | solution.py:88
  259.6 117.2 %all-gather.22.cloned.1.call-start = ((), (), s32[]{:S(2)}) async-start(), calls=%async_computation.17 | async-start | bytes 3145728 | tf_op jit(solution)/shard_map/all_gather | solution.py:92
  261.4 167.9 %all-gather.20.cloned.1.call-start = ((), (), s32[]{:S(2)}) async-start(), calls=%async_computation.15 | async-start | bytes 4456448 | tf_op jit(solution)/shard_map/all_gather | solution.py:129
  262.1 216.3 %reduce-scatter.16.cloned.1.call-start = ((), (), s32[]{:S(2)}) async-start(), calls=%async_computation.18 | async-start | bytes 3145728 | tf_op jit(solution)/shard_map/reduce_scatter | solution.py:113
  429.3 12.8 %copy-start.26 = (bf16[1024,2048]{1,0:T(8,128)(2,1)S(1)}, bf16[1024,2048]{1,0:T(8,128)(2,1)}, u32[]{:S(2)}) copy-start(bf16[1024,2048]{1,0:T(8,128)(2,1)} %all-gather.18.cloned.1.call-done) | copy-start | bytes 12582916
  447.9 64.6 %reduce-scatter.14.cloned.1.call-start = ((), (), s32[]{:S(2)}) async-start(), calls=%async_computation.16 | async-start | bytes 3145728 | tf_op jit(solution)/shard_map/reduce_scatter | solution.py:104
  457.2 95.5 %all-gather.24.cloned.1.call-start = ((), (), s32[]{:S(2)}) async-start(), calls=%async_computation.19 | async-start | bytes 3145728 | tf_op jit(solution)/shard_map/all_gather | solution.py:92
  518.2 34.5 %copy-start.11 = (bf16[8,64,1024]{2,1,0:T(8,128)(2,1)S(1)}, bf16[8,64,1024]{2,1,0:T(8,128)(2,1)}, u32[]{:S(2)}) copy-start(bf16[8,64,1024]{2,1,0:T(8,128)(2,1)} %copy-done.10) | copy-start | bytes 3145732
  518.2 34.5 %copy-start.29 = (bf16[512,1024]{0,1:T(8,128)(2,1)S(1)}, bf16[512,1024]{0,1:T(8,128)(2,1)}, u32[]{:S(2)}) copy-start(bf16[512,1024]{0,1:T(8,128)(2,1)} %all-gather.14.cloned.1.call-done) | copy-start | bytes 3145732
  519.5 131.8 %reduce-scatter.18.cloned.1.call-start = ((), (), s32[]{:S(2)}) async-start(), calls=%async_computation.20 | async-start | bytes 3145728 | tf_op jit(solution)/shard_map/reduce_scatter | solution.py:113
  602.2 10.6 copy-start.14
  602.2 10.6 copy-start.19
  618.2 108.7 %reduce-scatter.24.cloned.1.call-start = ((), (), s32[]{:S(2)}) async-start(), calls=%async_computation.23 | async-start | bytes 4456448 | tf_op jit(solution)/shard_map/reduce_scatter | solution.py:267
  628.1 174.4 %reduce-scatter.26.cloned.1.call-start = ((), (), s32[]{:S(2)}) async-start(), calls=%async_computation.24 | async-start | bytes 4456448 | tf_op jit(solution)/shard_map/reduce_scatter | solution.py:270
  637.5 225.0 %reduce-scatter.22.cloned.1.call-start = ((), (), s32[]{:S(2)}) async-start(), calls=%async_computation.22 | async-start | bytes 1114112 | tf_op jit(solution)/shard_map/reduce_scatter | solution.py:264
  640.1 4.3 copy-start.8
  644.1 355.4 %reduce-scatter.28.cloned.1.call-start = ((), (), s32[]{:S(2)}) async-start(), calls=%async_computation.25 | async-start | bytes 540672
  654.7 410.8 %reduce-scatter.20.cloned.1.call-start = ((), (), s32[]{:S(2)}) async-start(), calls=%async_computation.21 | async-start | bytes 3342336 | tf_op jit(solution)/shard_map/reduce_scatter | solution.py:261
  657.9 206.1 %copy-start.4 = (f32[512,1024]{1,0:T(8,128)S(1)}, f32[512,1024]{1,0:T(8,128)}, u32[]{:S(2)}) copy-start(f32[512,1024]{1,0:T(8,128)} %copy-done.3) | copy-start | bytes 6291460
  (16 other events, 31.0 us)
Sparse Core Ops, SparseCore 0:
  82.4 28.9 all-gather.9
  113.6 45.4 all-gather.11
  161.3 36.2 all-gather.13
  225.1 30.2 reduce-scatter.11
  257.4 50.3 all-gather.17
  309.8 31.6 all-gather.15
  343.6 33.0 all-gather.21
  378.9 50.3 all-gather.19
  448.0 30.4 reduce-scatter.15
  480.5 31.8 reduce-scatter.13
  519.6 33.0 all-gather.23
  618.3 31.8 reduce-scatter.17
  654.1 72.7 reduce-scatter.23
  730.6 71.7 reduce-scatter.25
  805.9 56.5 reduce-scatter.21
  864.7 134.8 reduce-scatter.27
  1003.2 62.2 reduce-scatter.19
where the time goes:
time: 1080 us; the launch traced here: 1070 us
  waiting for transfers between devices  748 us (69%)
  matrix products  165 us (15%)
  blocking collectives  71.4 us (7%)
  other arithmetic  59 us (5%)
  between operations  15.3 us (1%)
  local copies, waits for them, and re-layouts  13.2 us (1%)
    unnamed x18, waiting for transfers between devices  135 us
    reduce_scatter x1, waiting for transfers between devices, local(): lax.psum_scatter(grad_down.astype(jnp.bfloat16), 'dp', scatter_dimension=...  73.8 us
    all_gather x1, blocking collectives, local(): params = lax.all_gather(vectors, ('dp', 'tensor'), axis=1, tiled=True)  71.4 us
    reduce_scatter x1, waiting for transfers between devices, local(): lax.psum_scatter(grad_up.astype(jnp.bfloat16), 'dp', scatter_dimension=0,...  68.9 us
    reduce_scatter x1, waiting for transfers between devices, local(): lax.psum_scatter(grad_qkv_sum.astype(jnp.bfloat16), 'dp', scatter_dimensi...  64.6 us
    reduce_scatter x2, waiting for transfers between devices, branch_rows(): lax.psum_scatter(pair_sum(factor_pairs, matmul).astype(jnp.bfloat16), 'te...  61.3 us
    all_gather x2, waiting for transfers between devices, gather_rows(): return lax.all_gather(shard_low, 'tensor', axis=0, tiled=True)  60.5 us
    reduce_scatter x1, waiting for transfers between devices, local(): lax.psum_scatter(grad_proj_sum.astype(jnp.bfloat16), 'dp', scatter_dimens...  58.3 us
  transfers between devices with their start and end apart: 17, of which 15 were waited for; matrix products, arithmetic and copies ran while one was open for 12% of the time, Pallas kernels for 0%

commit v1 on v0

--- a/solution.py
+++ b/solution.py
@@ -9,6 +9,18 @@
 ROOT_HALF = 0.7071067811865476
 INV_ROOT_TAU = 0.3989422804014327
 MASKED = -1e30
+
+
+def collect(value, axis, dim):
+    ways, here, step = (lax.axis_size(axis), lax.axis_index(axis), value.shape[dim])
+    line, have = (value, 1)
+    while have < ways:
+        line = jnp.concatenate(
+            [line, lax.ppermute(line, axis, [(d, (d - have) % ways) for d in range(ways)])],
+            axis=dim,
+        )
+        have = 2 * have
+    return jnp.roll(line, here * step, axis=dim)
 
 
 def layer_norm(values):
@@ -89,7 +101,7 @@
 
 
 def gather_cotangent(shard_low):
-    return lax.all_gather(shard_low, "tensor", axis=0, tiled=True)
+    return collect(shard_low, "tensor", 0)
 
 
 def pair_sum(factor_pairs, product):

time: 1080 us -> 1040 us (0.963)
  waiting for transfers between devices: 748 us -> 688 us
  starting transfers between devices: 1.97 us -> 12.9 us
    all_gather x2 -> x0, waiting for transfers between devices: 58.3 us -> none  [gather_cotangent(): return lax.all_gather(shard_low, 'tensor', axis=0, tiled=True)]
    ppermute x0 -> x2, waiting for transfers between devices: none -> 49 us  [collect(): lax.ppermute(line, axis, [(d, (d - have) % ways) for d in range(ways)])]
    all_gather x1, waiting for transfers between devices: 45.6 us -> 4.42 us  [local(): lax.all_gather(up_weight, 'dp', axis=0, tiled=True)]
    reduce_scatter x2, starting transfers between devices: 0.08 us -> 11.1 us  [back_rows(): lax.psum_scatter(pair_sum(factor_pairs, times_transposed).astype(jnp.bflo...]
    unnamed x18 -> x16, waiting for transfers between devices: 135 us -> 135 us
  transfers between devices with their start and end apart: 17 -> 17, of which waited for: 15 -> 15; matrix products, arithmetic and copies ran while one was open for 12% -> 13% of each run, Pallas kernels for 0% -> 0%
where the time goes in v1:
time: 1040 us; the launch traced here: 1030 us
  waiting for transfers between devices  688 us (66%)
  matrix products  164 us (16%)
  blocking collectives  71.4 us (7%)
  other arithmetic  69 us (7%)
  between operations  15.4 us (1%)
  local copies, waits for them, and re-layouts  13.2 us (1%)
  starting transfers between devices  12.9 us (1%)
    unnamed x16, waiting for transfers between devices  135 us
    reduce_scatter x1, waiting for transfers between devices, local(): lax.psum_scatter(grad_down.astype(jnp.bfloat16), 'dp', scatter_dimension=...  73.8 us
    all_gather x1, blocking collectives, local(): params = lax.all_gather(vectors, ('dp', 'tensor'), axis=1, tiled=True)  71.4 us
    reduce_scatter x1, waiting for transfers between devices, local(): lax.psum_scatter(grad_up.astype(jnp.bfloat16), 'dp', scatter_dimension=0,...  69.2 us
    reduce_scatter x1, waiting for transfers between devices, local(): lax.psum_scatter(grad_qkv_sum.astype(jnp.bfloat16), 'dp', scatter_dimensi...  64.7 us
    reduce_scatter x2, waiting for transfers between devices, branch_rows(): lax.psum_scatter(pair_sum(factor_pairs, matmul).astype(jnp.bfloat16), 'te...  61.5 us
    all_gather x2, waiting for transfers between devices, gather_rows(): return lax.all_gather(shard_low, 'tensor', axis=0, tiled=True)  60.5 us
    reduce_scatter x1, waiting for transfers between devices, local(): lax.psum_scatter(grad_proj_sum.astype(jnp.bfloat16), 'dp', scatter_dimens...  58.4 us
  transfers between devices with their start and end apart: 17, of which 15 were waited for; matrix products, arithmetic and copies ran while one was open for 13% of the time, Pallas kernels for 0%

profile of v1, /device:TPU:0, one launch (start us, length us, event | category | flops | bytes accessed | tf_op | source)
XLA Modules:
  0.0 1033.3 jit_solution(15055348844627080580)
XLA Ops:
  7.2 71.4 %all-gather = f32[32,32,14]{1,2,0:T(8,128)S(1)} all-gather(f32[1,32,14]{1,2,0:T(8,128)} %bitcast.230), channel_id=1, replica_groups=mesh['dp'=16,'tensor'=2] {'dp','tensor'}, dimensions={0}, use_global_device_ids=true | all-gather | bytes 59136 | tf_op jit(solution)/shard_map/all_gather | solution.py:136
  84.5 26.9 %all-gather.8.cloned.1.call-done = bf16[1024,1024]{1,0:T(8,128)(2,1)} async-done(((bf16[512,1024]{1,0:T(8,128)(2,1)}), bf16[1024,1024]{1,0:T(8,128)(2,1)}) %all-gather.8.cloned.1.call-update) | async-done | bytes 2097168 | tf_op jit(solution)/shard_map/all_gather | solution.py:100
  111.4 47.7 %all-gather.10.cloned.1.call-done = bf16[3,1024,512]{2,1,0:T(8,128)(2,1)} async-done(((bf16[3,64,512]{2,1,0:T(8,128)(2,1)}), bf16[3,1024,512]{2,1,0:T(8,128)(2,1)}) %all-gather.10.cloned.1.call-update) | async-done | bytes 3145744 | tf_op jit(solution)/shard_map/all_gather | solution.py:138
  164.0 14.2 %fusion.1 = (f32[8,1024]{1,0:T(8,128)S(1)}, f32[8,1024,1024]{1,2,0:T(8,128)}) fusion(pred[1024]{0:T(1024)(128)(4,1)S(1)} %iota_compare_fusion, bf16[1024,8,64]{0,2,1:T(8,128)(2,1)S(1)} %bitcast.181, bf16[1024,8,64]{0,2,1:T(8,128)(2,1)S(1)} %bitcast.179), kind=kOutput, calls=%fused_computation.5 | convolution fusion | flops 1098899456 | bytes 35685376 | tf_op jit(solution)/shard_map/qhe,khe->hqk/dot_general | solution.py:62
  178.1 15.2 %exponential_reduce_fusion = f32[8,1024]{1,0:T(8,128)S(1)} fusion(f32[8,1024,1024]{1,2,0:T(8,128)} %get-tuple-element.35, f32[8,1024]{1,0:T(8,128)S(1)} %get-tuple-element.34, pred[1024]{0:T(1024)(128)(4,1)S(1)} %iota_compare_fusion), kind=kLoop, calls=%fused_computation.2 | loop fusion | flops 33546240 | bytes 33620992 | tf_op jit(solution)/shard_map/reduce_sum | solution.py:71
  193.3 5.3 copy-done
  198.6 9.5 fusion
  212.0 8.8 convolution_convert_fusion.10
  225.7 29.8 %reduce-scatter.12.cloned.1.call-done = bf16[512,1024]{1,0:T(8,128)(2,1)} async-done(((bf16[1024,1024]{1,0:T(8,128)(2,1)}), bf16[512,1024]{1,0:T(8,128)(2,1)}) %reduce-scatter.12.cloned.1.call-update) | async-done | bytes 1048592 | tf_op jit(solution)/shard_map/reduce_scatter | solution.py:116
  260.4 11.1 %reduce-scatter.16.cloned.1.call-start = ((), (), s32[]{:S(2)}) async-start(), calls=%async_computation.17 | async-start | bytes 3145728 | tf_op jit(solution)/shard_map/reduce_scatter | solution.py:125
  273.1 24.7 %collective-permute-done = bf16[512,1024]{1,0:T(8,128)(2,1)} collective-permute-done((bf16[512,1024]{1,0:T(8,128)(2,1)}, bf16[512,1024]{1,0:T(8,128)(2,1)}, u32[]{:S(2)}, u32[]{:S(2)}) %collective-permute-start) | collective-permute-done | bytes 1048608 | tf_op jit(solution)/shard_map/ppermute | solution.py:19
  297.8 5.8 fusion.39
  307.9 33.6 %all-gather.14.cloned.1.call-done = bf16[1024,1024]{1,0:T(8,128)(2,1)} async-done(((bf16[512,1024]{1,0:T(8,128)(2,1)}), bf16[1024,1024]{1,0:T(8,128)(2,1)}) %all-gather.14.cloned.1.call-update) | async-done | bytes 2097168 | tf_op jit(solution)/shard_map/all_gather | solution.py:100
  341.6 10.2 multiply_convert_fusion.1
  351.7 42.4 %all-gather.18.cloned.1.call-done = bf16[2048,1024]{0,1:T(8,128)(2,1)} async-done(((bf16[2048,64]{0,1:T(8,128)(2,1)}), bf16[2048,1024]{0,1:T(8,128)(2,1)}) %all-gather.18.cloned.1.call-update) | async-done | bytes 4194320 | tf_op jit(solution)/shard_map/all_gather | solution.py:141
  394.1 10.8 %fusion.56 = (f32[2048]{0:T(1024)S(1)}, bf16[1024,2048]{1,0:T(8,128)(2,1)S(1)}) fusion(f32[1024,2048]{1,0:T(8,128)} %get-tuple-element.37, f32[2048]{0:T(1024)S(1)} %dynamic_slice.14, bf16[1024,1024]{1,0:T(8,128)(2,1)} %fusion.39, bf16[2048,1024]{0,1:T(8,128)(2,1)} %all-gather.18.cloned.1.call-done), kind=kOutput, calls=%fused_computation.129 | convolution fusion | flops 4320131072 | bytes 18890752 | tf_op jit(solution)/shard_map/dot_general | solution.py:49
  406.9 5.8 fusion.45
  412.8 9.3 convolution_convert_fusion.2
  422.2 21.2 %reduce-scatter.16.cloned.1.call-done = bf16[512,1024]{1,0:T(8,128)(2,1)} async-done(((bf16[1024,1024]{1,0:T(8,128)(2,1)}), bf16[512,1024]{1,0:T(8,128)(2,1)}) %reduce-scatter.16.cloned.1.call-update) | async-done | bytes 1048592 | tf_op jit(solution)/shard_map/reduce_scatter | solution.py:125
  445.8 31.7 %reduce-scatter.14.cloned.1.call-done = bf16[512,1024]{1,0:T(8,128)(2,1)} async-done(((bf16[1024,1024]{1,0:T(8,128)(2,1)}), bf16[512,1024]{1,0:T(8,128)(2,1)}) %reduce-scatter.14.cloned.1.call-update) | async-done | bytes 1048592 | tf_op jit(solution)/shard_map/reduce_scatter | solution.py:116
  484.4 24.4 %collective-permute-done.1 = bf16[512,1024]{1,0:T(8,128)(2,1)S(1)} collective-permute-done((bf16[512,1024]{1,0:T(8,128)(2,1)S(1)}, bf16[512,1024]{1,0:T(8,128)(2,1)S(1)}, u32[]{:S(2)}, u32[]{:S(2)}) %collective-permute-start.1) | collective-permute-done | bytes 1048608 | tf_op jit(solution)/shard_map/ppermute | solution.py:19
  515.9 12.3 %bitcast_convert_fusion = (bf16[1024,8,64]{0,2,1:T(8,128)(2,1)}, f32[8,64,1024]{2,1,0:T(8,128)S(1)}) fusion(bf16[1024,8,64]{0,2,1:T(8,128)(2,1)} %bitcast.194, bf16[8,1024,1024]{1,2,0:T(8,128)(2,1)} %fusion), kind=kOutput, calls=%fused_computation.72 | convolution fusion | flops 1074266112 | bytes 20971520 | tf_op jit(solution)/shard_map/hqk,qhe->khe/dot_general | solution.py:80
  528.1 21.0 %multiply_convert_fusion = bf16[8,1024,1024]{1,2,0:T(8,128)(2,1)} fusion(f32[8,1024,1024]{1,2,0:T(8,128)} %get-tuple-element.35, f32[8,1024]{1,0:T(8,128)S(1)} %get-tuple-element.38, f32[8,1024]{1,0:T(8,128)S(1)} %log_add_fusion, pred[1024]{0:T(1024)(128)(4,1)S(1)} %iota_compare_fusion, bf16[1024,8,64]{0,2,1:T(8,128)(2,1)} %bitcast.195, ...), kind=kOutput, calls=%fused_computation | convolution fusion | flops 1124073472 | bytes 52495360 | tf_op jit(solution)/shard_map/qhe,khe->hqk/dot_general | solution.py:83
  549.2 12.3 %multiply_convert_fusion.2 = bf16[8,64,1024]{2,1,0:T(8,128)(2,1)} fusion(bf16[1024,8,64]{0,2,1:T(8,128)(2,1)} %bitcast.182, bf16[8,1024,1024]{1,2,0:T(8,128)(2,1)} %multiply_convert_fusion), kind=kOutput, calls=%fused_computation.78 | convolution fusion | flops 1074790400 | bytes 18874368 | tf_op jit(solution)/shard_map/hqk,qhe->khe/dot_general | solution.py:93
  561.5 10.6 %bitcast_convert_fusion.1 = (bf16[1024,8,64]{0,2,1:T(8,128)(2,1)S(1)}, f32[8,64,1024]{2,1,0:T(8,128)}) fusion(bf16[1024,8,64]{0,2,1:T(8,128)(2,1)} %bitcast.180, bf16[8,1024,1024]{1,2,0:T(8,128)(2,1)} %multiply_convert_fusion), kind=kOutput, calls=%fused_computation.74 | convolution fusion | flops 1074790400 | bytes 20971520 | tf_op jit(solution)/shard_map/hqk,khe->qhe/dot_general | solution.py:90
  577.7 9.4 convolution_convert_fusion.1
  587.1 9.3 convolution_convert_fusion
  616.9 69.2 %reduce-scatter.24.cloned.1.call-done = bf16[64,2048]{1,0:T(8,128)(2,1)} async-done(((bf16[1024,2048]{1,0:T(8,128)(2,1)}), bf16[64,2048]{1,0:T(8,128)(2,1)}) %reduce-scatter.24.cloned.1.call-update) | async-done | bytes 262160 | tf_op jit(solution)/shard_map/reduce_scatter | solution.py:279
  688.0 73.8 %reduce-scatter.26.cloned.1.call-done = bf16[2048,64]{0,1:T(8,128)(2,1)} async-done(((bf16[2048,1024]{0,1:T(8,128)(2,1)}), bf16[2048,64]{0,1:T(8,128)(2,1)}) %reduce-scatter.26.cloned.1.call-update) | async-done | bytes 262160 | tf_op jit(solution)/shard_map/reduce_scatter | solution.py:282
  763.5 58.4 %reduce-scatter.22.cloned.1.call-done = bf16[512,64]{0,1:T(8,128)(2,1)} async-done(((bf16[512,1024]{0,1:T(8,128)(2,1)}), bf16[512,64]{0,1:T(8,128)(2,1)}) %reduce-scatter.22.cloned.1.call-update) | async-done | bytes 65552 | tf_op jit(solution)/shard_map/reduce_scatter | solution.py:276
  826.7 132.0 %reduce-scatter.28.cloned.1.call-done = f32[32,14]{1,0:T(8,128)} async-done(((f32[1024,14]{1,0:T(8,128)}), f32[32,14]{1,0:T(8,128)}) %reduce-scatter.28.cloned.1.call-update) | async-done | bytes 1808
  960.1 64.7 %reduce-scatter.20.cloned.1.call-done = bf16[3,64,512]{2,1,0:T(8,128)(2,1)} async-done(((bf16[3,1024,512]{2,1,0:T(8,128)(2,1)}), bf16[3,64,512]{2,1,0:T(8,128)(2,1)}) %reduce-scatter.20.cloned.1.call-update) | async-done | bytes 196624 | tf_op jit(solution)/shard_map/reduce_scatter | solution.py:273
  (158 shorter events, 85.4 us)
Async XLA Ops:
  7.2 73.2 %copy-start.1 = (bf16[1,512,1024]{2,1,0:T(8,128)(2,1)S(1)}, bf16[1,512,1024]{2,1,0:T(8,128)(2,1)}, u32[]{:S(2)}) copy-start(bf16[1,512,1024]{2,1,0:T(8,128)(2,1)} %param.10) | copy-start | bytes 3145732
  7.2 104.2 %all-gather.8.cloned.1.call-start = ((), (), s32[]{:S(2)}) async-start(), calls=%async_computation.9 | async-start | bytes 3145728 | tf_op jit(solution)/shard_map/all_gather | solution.py:100
  78.9 3.3 copy-start.21
  80.8 81.6 %copy-start.25 = (f32[512]{0:T(512)}, f32[512]{0:T(512)S(1)}, u32[]{:S(2)}) copy-start(f32[512]{0:T(512)S(1)} %add_rsqrt_fusion.1) | copy-start | bytes 6148
  82.3 76.8 %all-gather.10.cloned.1.call-start = ((), (), s32[]{:S(2)}) async-start(), calls=%async_computation.10 | async-start | bytes 3342336 | tf_op jit(solution)/shard_map/all_gather | solution.py:138
  83.0 137.8 %all-gather.12.cloned.1.call-start = ((), (), s32[]{:S(2)}) async-start(), calls=%async_computation.11 | async-start | bytes 1114112 | tf_op jit(solution)/shard_map/all_gather | solution.py:139
  83.8 171.7 %reduce-scatter.12.cloned.1.call-start = ((), (), s32[]{:S(2)}) async-start(), calls=%async_computation.12 | async-start | bytes 3145728 | tf_op jit(solution)/shard_map/reduce_scatter | solution.py:116
  159.1 3.5 copy-start.28
  163.9 14.2 %copy-start.6 = (bf16[1024,512]{0,1:T(8,128)(2,1)}, bf16[1024,512]{0,1:T(8,128)(2,1)S(1)}, u32[]{:S(2)}) copy-start(bf16[1024,512]{0,1:T(8,128)(2,1)S(1)} %add_convert_fusion.3) | copy-start | bytes 3145732
  178.1 20.5 %copy-start = (f32[8,1024,1024]{1,2,0:T(8,128)S(1)}, f32[8,1024,1024]{1,2,0:T(8,128)}, u32[]{:S(2)}) copy-start(f32[8,1024,1024]{1,2,0:T(8,128)} %get-tuple-element.35) | copy-start | bytes 100663296
  220.8 4.3 copy-start.11
  225.1 82.8 %all-gather.16.cloned.1.call-start = ((), (), s32[]{:S(2)}) async-start(), calls=%async_computation.14 | async-start | bytes 4456448 | tf_op jit(solution)/shard_map/all_gather | solution.py:140
  225.7 115.9 %all-gather.14.cloned.1.call-start = ((), (), s32[]{:S(2)}) async-start(), calls=%async_computation.13 | async-start | bytes 3145728 | tf_op jit(solution)/shard_map/all_gather | solution.py:100
  258.0 13.5 %copy-start.9 = (bf16[1,512,1024]{2,1,0:T(8,128)(2,1)S(1)}, bf16[1,512,1024]{2,1,0:T(8,128)(2,1)}, u32[]{:S(2)}) copy-start(bf16[1,512,1024]{2,1,0:T(8,128)(2,1)} %param.17) | copy-start | bytes 3145732
  259.6 134.5 %all-gather.18.cloned.1.call-start = ((), (), s32[]{:S(2)}) async-start(), calls=%async_computation.15 | async-start | bytes 4456448 | tf_op jit(solution)/shard_map/all_gather | solution.py:141
  260.4 182.9 %reduce-scatter.16.cloned.1.call-start = ((), (), s32[]{:S(2)}) async-start(), calls=%async_computation.17 | async-start | bytes 3145728 | tf_op jit(solution)/shard_map/reduce_scatter | solution.py:125
  272.7 25.1 %collective-permute-start = (bf16[512,1024]{1,0:T(8,128)(2,1)}, bf16[512,1024]{1,0:T(8,128)(2,1)}, u32[]{:S(2)}, u32[]{:S(2)}) collective-permute-start(bf16[512,1024]{1,0:T(8,128)(2,1)} %fusion.20), channel_id=1, source_target_pairs={{0,1},{1,0},{2,3},{3,2},{4,5},{5,4},{6,7},{7,6},{8,9},{9,8},{10,11... | collective-permute-start | bytes 3145736 | tf_op jit(solution)/shard_map/ppermute | solution.py:19
  394.1 12.8 %copy-start.27 = (bf16[1024,2048]{1,0:T(8,128)(2,1)S(1)}, bf16[1024,2048]{1,0:T(8,128)(2,1)}, u32[]{:S(2)}) copy-start(bf16[1024,2048]{1,0:T(8,128)(2,1)} %all-gather.16.cloned.1.call-done) | copy-start | bytes 12582916
  412.7 64.8 %reduce-scatter.14.cloned.1.call-start = ((), (), s32[]{:S(2)}) async-start(), calls=%async_computation.16 | async-start | bytes 3145728 | tf_op jit(solution)/shard_map/reduce_scatter | solution.py:116
  422.1 188.1 %reduce-scatter.18.cloned.1.call-start = ((), (), s32[]{:S(2)}) async-start(), calls=%async_computation.18 | async-start | bytes 3145728 | tf_op jit(solution)/shard_map/reduce_scatter | solution.py:125
  483.9 29.6 %copy-start.12 = (bf16[8,64,1024]{2,1,0:T(8,128)(2,1)S(1)}, bf16[8,64,1024]{2,1,0:T(8,128)(2,1)}, u32[]{:S(2)}) copy-start(bf16[8,64,1024]{2,1,0:T(8,128)(2,1)} %copy-done.11) | copy-start | bytes 3145732
  483.9 29.6 %copy-start.30 = (bf16[512,1024]{0,1:T(8,128)(2,1)S(1)}, bf16[512,1024]{0,1:T(8,128)(2,1)}, u32[]{:S(2)}) copy-start(bf16[512,1024]{0,1:T(8,128)(2,1)} %all-gather.12.cloned.1.call-done) | copy-start | bytes 3145732
  484.0 24.8 %collective-permute-start.1 = (bf16[512,1024]{1,0:T(8,128)(2,1)S(1)}, bf16[512,1024]{1,0:T(8,128)(2,1)S(1)}, u32[]{:S(2)}, u32[]{:S(2)}) collective-permute-start(bf16[512,1024]{1,0:T(8,128)(2,1)S(1)} %multiply_convert_fusion.3), channel_id=1, source_target_pairs={{0,1},{1,0},{2,3},{3,2},{4,5},{5,4},{6,7},{7,6},{8,9},{9,8},{10,11... | collective-permute-start | bytes 3145736 | tf_op jit(solution)/shard_map/ppermute | solution.py:19
  561.4 10.6 %copy-start.15 = (bf16[8,64,1024]{2,1,0:T(8,128)(2,1)S(1)}, bf16[8,64,1024]{2,1,0:T(8,128)(2,1)}, u32[]{:S(2)}) copy-start(bf16[8,64,1024]{2,1,0:T(8,128)(2,1)} %multiply_convert_fusion.2) | copy-start | bytes 3145732
  561.4 10.6 %copy-start.20 = (bf16[3,1024,512]{2,1,0:T(8,128)(2,1)S(1)}, bf16[3,1024,512]{2,1,0:T(8,128)(2,1)}, u32[]{:S(2)}) copy-start(bf16[3,1024,512]{2,1,0:T(8,128)(2,1)} %all-gather.10.cloned.1.call-done) | copy-start | bytes 9437188
  577.4 108.8 %reduce-scatter.24.cloned.1.call-start = ((), (), s32[]{:S(2)}) async-start(), calls=%async_computation.21 | async-start | bytes 4456448 | tf_op jit(solution)/shard_map/reduce_scatter | solution.py:279
  587.0 174.7 %reduce-scatter.26.cloned.1.call-start = ((), (), s32[]{:S(2)}) async-start(), calls=%async_computation.22 | async-start | bytes 4456448 | tf_op jit(solution)/shard_map/reduce_scatter | solution.py:282
  596.5 225.5 %reduce-scatter.22.cloned.1.call-start = ((), (), s32[]{:S(2)}) async-start(), calls=%async_computation.20 | async-start | bytes 1114112 | tf_op jit(solution)/shard_map/reduce_scatter | solution.py:276
  599.0 4.4 copy-start.8
  603.0 355.7 %reduce-scatter.28.cloned.1.call-start = ((), (), s32[]{:S(2)}) async-start(), calls=%async_computation.23 | async-start | bytes 540672
  613.6 411.2 %reduce-scatter.20.cloned.1.call-start = ((), (), s32[]{:S(2)}) async-start(), calls=%async_computation.19 | async-start | bytes 3342336 | tf_op jit(solution)/shard_map/reduce_scatter | solution.py:273
  616.9 206.5 %copy-start.4 = (f32[512,1024]{1,0:T(8,128)S(1)}, f32[512,1024]{1,0:T(8,128)}, u32[]{:S(2)}) copy-start(f32[512,1024]{1,0:T(8,128)} %copy-done.3) | copy-start | bytes 6291460
  (17 other events, 34.4 us)
Sparse Core Ops, SparseCore 0:
  82.4 28.9 all-gather.7
  113.6 45.4 all-gather.9
  161.3 36.1 all-gather.11
  225.2 30.2 reduce-scatter.11
  257.5 50.3 all-gather.15
  309.9 31.6 all-gather.13
  343.7 50.3 all-gather.17
  412.8 30.4 reduce-scatter.15
  445.6 31.8 reduce-scatter.13
  577.5 31.8 reduce-scatter.17
  613.3 72.8 reduce-scatter.23
  689.9 71.8 reduce-scatter.25
  765.4 56.5 reduce-scatter.21
  824.0 134.6 reduce-scatter.27
  962.4 62.3 reduce-scatter.19
